TPU v7x, 512 devices: a whole 4x4x16 slice. The times are simulated.
512 devices in a mesh: ctx: 64 (over z_hi, x, y), head: 8 (over z_lo, core).
Axes of the slice: x: 4, y: 4, z: 16 (z_hi: 4, z_lo: 4; z = z_hi * 4 + z_lo), core: 2. Of those that a mesh axis runs over, the one named last changes fastest.
Arguments:
- queries: bfloat16 [16384, 6144], P(('ctx', 'head')), may hold values from -32 to 32
- keys: bfloat16 [16384, 6144], P(('ctx', 'head')), may hold values from -12 to 12
- values: bfloat16 [16384, 6144], P(('ctx', 'head')), may hold values from -6 to 6
- cache_keys: bfloat16 [32768, 6144], P('ctx', 'head'), may hold values from -6 to 6
- cache_values: bfloat16 [32768, 6144], P('ctx', 'head'), may hold values from -6 to 6
- pattern: int32 [128, 4], replicated, may hold values from 0 to 255, as said below
- reached: int32 [128], replicated, may hold values from 1 to 4, as said below
- gate: float32 [6144], replicated, may hold values from 0.5 to 2
Outputs:
- mixed: bfloat16 [16384, 6144], P(('ctx', 'head'))
Inputs may be any that keep to these rules, and one draw needn't show every extreme that they name: `pattern`: every entry of row g names a cached tile of ctx index g // 2 - 1, g // 2 or g // 2 + 1, where ctx index c holds cached tiles c * 4 to (c + 1) * 4 - 1. Only the first reached[g] entries of row g of pattern are used.
All inputs are finite; a program needn't handle non-finite values.
Results may differ from a plain program's by a relative error of at most 0.011.
Values may be sent and summed in bfloat16 or wider, within the bound.
No kernel may reach another device: no remote copies, remote signals or barrier semaphores. Data moves between devices by JAX's collectives and lax.ppermute only.
A program may use at most 64 MiB of HBM per device.

v0:
```python
import jax
import jax.numpy as jnp
from jax import lax
from jax.sharding import PartitionSpec as P

HD = 128
TILE = 128
REACH = 4
NEGATIVE = -1e30


def with_halo(block, sides, width):
    for axis, dim in sides:
        count = lax.axis_size(axis)
        forward = [(i, i + 1) for i in range(count - 1)]
        backward = [(target, source) for source, target in forward]
        low = lax.ppermute(
            lax.slice_in_dim(block, block.shape[dim] - width, None, axis=dim), axis, forward
        )
        high = lax.ppermute(lax.slice_in_dim(block, 0, width, axis=dim), axis, backward)
        block = jnp.concatenate([low, block, high], axis=dim)
    return block


def tile_attend(q_tile, key_blocks, value_blocks, usable_keys):
    scores = jnp.einsum(
        "qhd,nkhd->hqnk", q_tile, key_blocks, preferred_element_type=jnp.float32
    ) * q_tile.shape[2] ** (-0.5)
    keep_mask = usable_keys[None, None, :, None]
    scores = jnp.where(keep_mask, scores, NEGATIVE)
    row_peak = jnp.max(scores, axis=(2, 3))
    expos = jnp.exp(scores - row_peak[:, :, None, None])
    row_total = jnp.sum(expos, axis=(2, 3))
    weights = expos.astype(jnp.bfloat16)
    summed = jnp.einsum("hqnk,nkhd->qhd", weights, value_blocks, preferred_element_type=jnp.float32)
    return (summed, row_peak, row_total)


def finish(portions):
    overall_peak = portions[0][1]
    numerator = 0.0
    denominator = 0.0
    for portion in portions:
        factor = jnp.exp(portion[1] - overall_peak)
        denominator = denominator + factor * portion[2]
        numerator = numerator + portion[0] * jnp.transpose(factor, (0, 2, 1))[..., None]
    return numerator / jnp.transpose(denominator, (0, 2, 1))[..., None]


def local(queries, keys, values, cache_keys, cache_values, pattern, reached, gate):
    local_q, local_k, local_v = (
        lax.all_to_all(queries, "head", split_axis=1, concat_axis=0, tiled=True),
        lax.all_to_all(keys, "head", split_axis=1, concat_axis=0, tiled=True),
        lax.all_to_all(values, "head", split_axis=1, concat_axis=0, tiled=True),
    )
    rows = local_q.shape[0]
    width = local_q.shape[1]
    heads_here = width // HD
    tiles_here = rows // TILE
    ctx_count = lax.axis_size("ctx")
    ctx_index = lax.axis_index("ctx")
    all_tiles = ctx_count * tiles_here
    first_tile = ctx_index * tiles_here
    cache_tiles = cache_keys.shape[0] // TILE
    rim_blocks = with_halo(jnp.stack([local_k, local_v]), (("ctx", 1),), 2 * TILE)
    tile_ids = first_tile + jnp.arange(tiles_here, dtype=jnp.int32)
    near_ids = tile_ids[:, None] + jnp.arange(-2, 3, dtype=jnp.int32)[None, :]
    group_valid = (near_ids >= 0) & (near_ids < all_tiles)
    own_pattern = lax.dynamic_slice_in_dim(pattern, first_tile, tiles_here, 0)
    own_reached = lax.dynamic_slice_in_dim(reached, first_tile, tiles_here, 0)
    slot_ids = jnp.arange(REACH, dtype=jnp.int32)
    cache_stack = jnp.stack([cache_keys, cache_values])

    def query_tile(block_q, tile_index):
        return lax.dynamic_slice_in_dim(block_q, tile_index * TILE, TILE, 0).reshape(
            TILE, heads_here, HD
        )

    def group_blocks(tile_index):
        window = lax.dynamic_slice_in_dim(rim_blocks, tile_index * TILE, 5 * TILE, 1)
        return window.reshape(2, 5, TILE, heads_here, HD)

    widened = with_halo(cache_stack, (("ctx", 1),), cache_keys.shape[0])
    widened = widened.reshape(2, 3 * cache_tiles, TILE, heads_here, HD)

    def one_tile(tile_index):
        local_ids = own_pattern[tile_index] - (ctx_index - 1) * cache_tiles
        picked = jnp.take(widened, local_ids, axis=1)
        blocks = jnp.concatenate([group_blocks(tile_index), picked], axis=1)
        usable_keys = jnp.concatenate([group_valid[tile_index], slot_ids < own_reached[tile_index]])
        return tile_attend(query_tile(local_q, tile_index), blocks[0], blocks[1], usable_keys)

    attended = finish([lax.map(one_tile, jnp.arange(tiles_here, dtype=jnp.int32))])
    gate_part = lax.dynamic_slice_in_dim(gate, lax.axis_index("head") * width, width, 0)
    gated = (attended.reshape(rows, width) * gate_part).astype(jnp.bfloat16)
    return lax.all_to_all(gated, "head", split_axis=0, concat_axis=1, tiled=True)


def solution(mesh):
    placed = (
        P(("ctx", "head"), None),
        P(("ctx", "head"), None),
        P(("ctx", "head"), None),
        P("ctx", "head"),
        P("ctx", "head"),
        P(),
        P(),
        P(),
    )
    return jax.shard_map(
        local, mesh=mesh, in_specs=placed, out_specs=P(("ctx", "head"), None), check_vma=False
    )
```

profile of v0, /device:TPU:256, one launch (start us, length us, event | category | flops | bytes accessed | tf_op | source)
XLA Modules:
  0.0 328.4 jit_solution(431748586827617101)
XLA Ops:
  0.0 1.9 copy.82
  1.9 3.6 %all-to-all-start = ((bf16[32,8,768]{2,0,1:T(8,128)(2,1)}), bf16[32,8,768]{2,0,1:T(8,128)(2,1)S(1)}, u32[]{:S(2)}, u32[]{:S(2)}) async-start(bf16[32,8,768]{2,0,1:T(8,128)(2,1)} %bitcast.70), calls=%async_computation | async-start | bytes 786432 | tf_op jit(solution)/shard_map/all_to_all | solution.py:53
  5.5 1.8 copy.81
  7.3 10.7 %all-to-all-done = bf16[32,8,768]{2,0,1:T(8,128)(2,1)S(1)} async-done(((bf16[32,8,768]{2,0,1:T(8,128)(2,1)}), bf16[32,8,768]{2,0,1:T(8,128)(2,1)S(1)}, u32[]{:S(2)}, u32[]{:S(2)}) %all-to-all-start) | async-done | bytes 393248 | tf_op jit(solution)/shard_map/all_to_all | solution.py:53
  18.0 3.5 %all-to-all-start.1 = ((bf16[32,8,768]{2,0,1:T(8,128)(2,1)}), bf16[32,8,768]{2,0,1:T(8,128)(2,1)S(1)}, u32[]{:S(2)}, u32[]{:S(2)}) async-start(bf16[32,8,768]{2,0,1:T(8,128)(2,1)} %bitcast.69), calls=%async_computation.1 | async-start | bytes 786432 | tf_op jit(solution)/shard_map/all_to_all | solution.py:54
  22.8 3.5 %collective-permute-start.2 = (bf16[2,512,768]{2,1,0:T(8,128)(2,1)}, bf16[2,512,768]{2,1,0:T(8,128)(2,1)}, u32[]{:S(2)}, u32[]{:S(2)}) collective-permute-start(bf16[2,512,768]{2,1,0:T(8,128)(2,1)} %pad_maximum_fusion.3), channel_id=1, source_target_pairs={{0,8},{8,16},{16,24},{24,32},{32,40},{40,48},{48,56},{56,64},{64,7... | collective-permute-start | bytes 4718600 | tf_op jit(solution)/shard_map/ppermute | solution.py:17
  26.2 10.5 %collective-permute-start.3 = (bf16[2,512,768]{2,1,0:T(8,128)(2,1)}, bf16[2,512,768]{2,1,0:T(8,128)(2,1)}, u32[]{:S(2)}, u32[]{:S(2)}) collective-permute-start(bf16[2,512,768]{2,1,0:T(8,128)(2,1)} %pad_maximum_fusion.3), channel_id=1, source_target_pairs={{8,0},{16,8},{24,16},{32,24},{40,32},{48,40},{56,48},{64,56},{72,6... | collective-permute-start | bytes 4718600 | tf_op jit(solution)/shard_map/ppermute | solution.py:20
  37.5 5.0 %all-to-all-start.2 = ((bf16[32,8,768]{2,0,1:T(8,128)(2,1)}), bf16[32,8,768]{2,0,1:T(8,128)(2,1)S(1)}, u32[]{:S(2)}, u32[]{:S(2)}) async-start(bf16[32,8,768]{2,0,1:T(8,128)(2,1)} %bitcast.68), calls=%async_computation.2 | async-start | bytes 786432 | tf_op jit(solution)/shard_map/all_to_all | solution.py:52
  44.6 1.9 collective-permute-start
  46.5 37.1 %collective-permute-start.1 = (bf16[2,256,768]{2,1,0:T(8,128)(2,1)}, bf16[2,256,768]{2,1,0:T(8,128)(2,1)}, u32[]{:S(2)}, u32[]{:S(2)}) collective-permute-start(bf16[2,256,768]{2,1,0:T(8,128)(2,1)} %pad_maximum_fusion.4), channel_id=1, source_target_pairs={{8,0},{16,8},{24,16},{32,24},{40,32},{48,40},{56,48},{64,56},{72,6... | collective-permute-start | bytes 2359304 | tf_op jit(solution)/shard_map/ppermute | solution.py:20
  83.7 128.9 %collective-permute-done.3 = bf16[2,512,768]{2,1,0:T(8,128)(2,1)} collective-permute-done((bf16[2,512,768]{2,1,0:T(8,128)(2,1)}, bf16[2,512,768]{2,1,0:T(8,128)(2,1)}, u32[]{:S(2)}, u32[]{:S(2)}) %collective-permute-start.3) | collective-permute-done | bytes 1572896 | tf_op jit(solution)/shard_map/ppermute | solution.py:20
  212.6 4.9 %pad_maximum_fusion.1 = bf16[2,1536,768]{2,1,0:T(8,128)(2,1)} fusion(bf16[2,512,768]{2,1,0:T(8,128)(2,1)} %collective-permute-done.3, bf16[1,512,768]{2,1,0:T(8,128)(2,1)S(1)} %bitcast.112, bf16[1,512,768]{2,1,0:T(8,128)(2,1)S(1)} %bitcast.114, bf16[2,512,768]{2,1,0:T(8,128)(2,1)} %collective-permute-done.2), kind=kLoop, calls=%fused_computation.38 | loop fusion | flops 18874368 | bytes 9437184 | tf_op jit(solution)/shard_map/concatenate | solution.py:21
  217.5 10.8 %reshape.82 = bf16[2,12,128,6,128]{4,3,2,1,0:T(8,128)(2,1)} reshape(bf16[2,1536,768]{2,1,0:T(8,128)(2,1)} %pad_maximum_fusion.1) | data formatting | bytes 9437184 | tf_op jit(solution)/shard_map/reshape | solution.py:84
  228.3 6.4 %copy.60 = bf16[2,12,128,6,128]{4,2,3,1,0:T(8,128)(2,1)} copy(bf16[2,12,128,6,128]{4,3,2,1,0:T(8,128)(2,1)} %reshape.82) | data formatting | bytes 9437184
  234.7 13.2 %collective-permute-done = bf16[2,256,768]{2,1,0:T(8,128)(2,1)} collective-permute-done((bf16[2,256,768]{2,1,0:T(8,128)(2,1)}, bf16[2,256,768]{2,1,0:T(8,128)(2,1)}, u32[]{:S(2)}, u32[]{:S(2)}) %collective-permute-start) | collective-permute-done | bytes 786464 | tf_op jit(solution)/shard_map/ppermute | solution.py:17
  247.9 3.0 pad_maximum_fusion.2
  250.9 47.6 %while.17 = (s32[]{:T(128)}, f32[2,128,6,128]{1,3,2,0:T(8,128)}, f32[2,6,128]{2,1,0:T(8,128)S(1)}, f32[2,6,128]{2,1,0:T(8,128)S(1)}, s32[2]{0:T(128)S(1)}, /*ind...) while((s32[]{:T(128)}, f32[2,128,6,128]{1,3,2,0:T(8,128)}, ...), condition=%wide.region_3.4_spmd.clone, body=%wide.region_0.3_spmd.clone.sunk | while | flops 465272384 | bytes 78874744 | solution.py:93
  253.6 3.2 gather_fusion
  258.9 2.9 constant_dynamic-slice_fusion.6
  261.9 4.2 %reshape.105 = bf16[2,5,128,6,128]{4,3,2,1,0:T(8,128)(2,1)S(1)} reshape(bf16[2,640,768]{2,1,0:T(8,128)(2,1)} %constant_dynamic-slice_fusion.6) | data formatting | bytes 3932160 | tf_op jit(solution)/shard_map/while/body/eval_jaxpr/reshape | solution.py:81
  277.4 3.2 gather_fusion
  282.7 2.9 constant_dynamic-slice_fusion.6
  285.7 4.2 %reshape.105 = bf16[2,5,128,6,128]{4,3,2,1,0:T(8,128)(2,1)S(1)} reshape(bf16[2,640,768]{2,1,0:T(8,128)(2,1)} %constant_dynamic-slice_fusion.6) | data formatting | bytes 3932160 | tf_op jit(solution)/shard_map/while/body/eval_jaxpr/reshape | solution.py:81
  300.4 27.2 %all_to_all.67 = bf16[8,32,768]{2,1,0:T(8,128)(2,1)S(1)} all-to-all(bf16[8,32,768]{2,1,0:T(8,128)(2,1)S(1)} %multiply_convert_fusion), channel_id=1, replica_groups=mesh['ctx'=64,'head'=8] {'head'}, dimensions={0} | all-to-all | bytes 786432 | tf_op jit(solution)/shard_map/all_to_all | solution.py:96
  (94 shorter events, 28.0 us)
Async XLA Ops:
  0.0 42.5 %copy-start = (s32[128,4]{0,1:T(4,128)S(1)}, s32[128,4]{0,1:T(4,128)}, u32[]{:S(2)}) copy-start(s32[128,4]{0,1:T(4,128)} %param.15) | copy-start | bytes 6148
  0.0 21.4 %copy-start.6 = (bf16[512,768]{1,0:T(8,128)(2,1)S(1)}, bf16[512,768]{1,0:T(8,128)(2,1)}, u32[]{:S(2)}) copy-start(bf16[512,768]{1,0:T(8,128)(2,1)} %param.13) | copy-start | bytes 2359300
  0.0 21.4 %copy-start.5 = (bf16[512,768]{1,0:T(8,128)(2,1)S(1)}, bf16[512,768]{1,0:T(8,128)(2,1)}, u32[]{:S(2)}) copy-start(bf16[512,768]{1,0:T(8,128)(2,1)} %param.14) | copy-start | bytes 2359300
  0.0 36.7 %copy-start.9 = (bf16[32,6144]{1,0:T(8,128)(2,1)S(1)}, bf16[32,6144]{1,0:T(8,128)(2,1)}, u32[]{:S(2)}) copy-start(bf16[32,6144]{1,0:T(8,128)(2,1)} %param.10) | copy-start | bytes 1179652
  1.9 40.8 %copy-start.10 = (s32[128]{0:T(128)S(1)}, s32[128]{0:T(128)}, u32[]{:S(2)}) copy-start(s32[128]{0:T(128)} %param.16) | copy-start | bytes 1540
  1.9 16.0 %all-to-all-start = ((bf16[32,8,768]{2,0,1:T(8,128)(2,1)}), bf16[32,8,768]{2,0,1:T(8,128)(2,1)S(1)}, u32[]{:S(2)}, u32[]{:S(2)}) async-start(bf16[32,8,768]{2,0,1:T(8,128)(2,1)} %bitcast.70), calls=%async_computation | async-start | bytes 786432 | tf_op jit(solution)/shard_map/all_to_all | solution.py:53
  18.0 19.5 %all-to-all-start.1 = ((bf16[32,8,768]{2,0,1:T(8,128)(2,1)}), bf16[32,8,768]{2,0,1:T(8,128)(2,1)S(1)}, u32[]{:S(2)}, u32[]{:S(2)}) async-start(bf16[32,8,768]{2,0,1:T(8,128)(2,1)} %bitcast.69), calls=%async_computation.1 | async-start | bytes 786432 | tf_op jit(solution)/shard_map/all_to_all | solution.py:54
  22.8 60.9 %collective-permute-start.2 = (bf16[2,512,768]{2,1,0:T(8,128)(2,1)}, bf16[2,512,768]{2,1,0:T(8,128)(2,1)}, u32[]{:S(2)}, u32[]{:S(2)}) collective-permute-start(bf16[2,512,768]{2,1,0:T(8,128)(2,1)} %pad_maximum_fusion.3), channel_id=1, source_target_pairs={{0,8},{8,16},{16,24},{24,32},{32,40},{40,48},{48,56},{56,64},{64,7... | collective-permute-start | bytes 4718600 | tf_op jit(solution)/shard_map/ppermute | solution.py:17
  26.2 186.4 %collective-permute-start.3 = (bf16[2,512,768]{2,1,0:T(8,128)(2,1)}, bf16[2,512,768]{2,1,0:T(8,128)(2,1)}, u32[]{:S(2)}, u32[]{:S(2)}) collective-permute-start(bf16[2,512,768]{2,1,0:T(8,128)(2,1)} %pad_maximum_fusion.3), channel_id=1, source_target_pairs={{8,0},{16,8},{24,16},{32,24},{40,32},{48,40},{56,48},{64,56},{72,6... | collective-permute-start | bytes 4718600 | tf_op jit(solution)/shard_map/ppermute | solution.py:20
  37.5 213.4 %all-to-all-start.2 = ((bf16[32,8,768]{2,0,1:T(8,128)(2,1)}), bf16[32,8,768]{2,0,1:T(8,128)(2,1)S(1)}, u32[]{:S(2)}, u32[]{:S(2)}) async-start(bf16[32,8,768]{2,0,1:T(8,128)(2,1)} %bitcast.68), calls=%async_computation.2 | async-start | bytes 786432 | tf_op jit(solution)/shard_map/all_to_all | solution.py:52
  44.6 203.4 %collective-permute-start = (bf16[2,256,768]{2,1,0:T(8,128)(2,1)}, bf16[2,256,768]{2,1,0:T(8,128)(2,1)}, u32[]{:S(2)}, u32[]{:S(2)}) collective-permute-start(bf16[2,256,768]{2,1,0:T(8,128)(2,1)} %pad_maximum_fusion.4), channel_id=1, source_target_pairs={{0,8},{8,16},{16,24},{24,32},{32,40},{40,48},{48,56},{56,64},{64,7... | collective-permute-start | bytes 2359304 | tf_op jit(solution)/shard_map/ppermute | solution.py:17
  46.5 201.5 %collective-permute-start.1 = (bf16[2,256,768]{2,1,0:T(8,128)(2,1)}, bf16[2,256,768]{2,1,0:T(8,128)(2,1)}, u32[]{:S(2)}, u32[]{:S(2)}) collective-permute-start(bf16[2,256,768]{2,1,0:T(8,128)(2,1)} %pad_maximum_fusion.4), channel_id=1, source_target_pairs={{8,0},{16,8},{24,16},{32,24},{40,32},{48,40},{56,48},{64,56},{72,6... | collective-permute-start | bytes 2359304 | tf_op jit(solution)/shard_map/ppermute | solution.py:20
  266.1 1.8 copy-start.3
  266.6 1.3 copy-start.1
  270.3 1.5 copy-start.2
  270.3 2.0 copy-start.4
  270.3 2.2 copy-start.7
  273.8 0.9 copy-start.8
  289.9 1.8 copy-start.3
  290.4 1.3 copy-start.1
  294.1 1.5 copy-start.2
  294.1 2.0 copy-start.4
  294.1 2.2 copy-start.7
  297.6 0.9 copy-start.8
where the time goes:
time: 330 us; the launch traced here: 328 us
  waiting for transfers between devices  153 us (46%)
  starting transfers between devices  65 us (20%)
  local copies, waits for them, and re-layouts  54.7 us (17%)
  blocking collectives  27.2 us (8%)
  other arithmetic  18.8 us (6%)
  loops' own time  5.72 us (2%)
  matrix products  3.93 us (1%)
    ppermute x2, waiting for transfers between devices, with_halo(): lax.ppermute(lax.slice_in_dim(block, 0, width, axis=dim), axis, backward)  129 us
    ppermute x2, starting transfers between devices, with_halo(): lax.ppermute(lax.slice_in_dim(block, 0, width, axis=dim), axis, backward)  47.6 us
    all_to_all x1, blocking collectives, local(): lax.all_to_all(gated, 'head', split_axis=0, concat_axis=1, tiled=True)  27.2 us
    ppermute x2, waiting for transfers between devices, with_halo(): lax.ppermute(lax.slice_in_dim(block, block.shape[dim] - width, None, axis...  13.2 us
    reshape x1, local copies, waits for them, and re-layouts, local(): widened = widened.reshape(2, 3 * cache_tiles, TILE, heads_here, HD)  10.8 us
    all_to_all x1, waiting for transfers between devices, local(): lax.all_to_all(keys, 'head', split_axis=1, concat_axis=0, tiled=True)  10.7 us
    reshape x4, local copies, waits for them, and re-layouts, group_blocks(): return window.reshape(2, 5, TILE, heads_here, HD)  9.41 us
    concatenate x2, other arithmetic, with_halo(): block = jnp.concatenate([low, block, high], axis=dim)  7.87 us
  transfers between devices with their start and end apart: 7, of which 3 were waited for; matrix products, arithmetic and copies ran while one was open for 9% of the time, Pallas kernels for 0%

commit v1 on v0

--- a/solution.py
+++ b/solution.py
@@ -50,7 +50,10 @@
 def local(queries, keys, values, cache_keys, cache_values, pattern, reached, gate):
     local_q, local_k, local_v = (
         lax.all_to_all(queries, "head", split_axis=1, concat_axis=0, tiled=True),
-        lax.all_to_all(keys, "head", split_axis=1, concat_axis=0, tiled=True),
+        jnp.concatenate(
+            lax.all_to_all(jnp.stack(jnp.split(keys, lax.axis_size("head"), axis=1)), "head", 0, 0),
+            axis=0,
+        ),
         lax.all_to_all(values, "head", split_axis=1, concat_axis=0, tiled=True),
     )
     rows = local_q.shape[0]

time: 330 us -> 340 us (1.030)
  local copies, waits for them, and re-layouts: 54.7 us -> 64.3 us
    unnamed x12 -> x19, local copies, waits for them, and re-layouts: 6.55 us -> 16.6 us
where the time goes in v1:
time: 340 us; the launch traced here: 338 us
  waiting for transfers between devices  153 us (45%)
  starting transfers between devices  65 us (19%)
  local copies, waits for them, and re-layouts  64.3 us (19%)
  blocking collectives  27.2 us (8%)
  other arithmetic  18.8 us (6%)
  loops' own time  5.72 us (2%)
  matrix products  3.93 us (1%)
    ppermute x2, waiting for transfers between devices, with_halo(): lax.ppermute(lax.slice_in_dim(block, 0, width, axis=dim), axis, backward)  129 us
    ppermute x2, starting transfers between devices, with_halo(): lax.ppermute(lax.slice_in_dim(block, 0, width, axis=dim), axis, backward)  47.6 us
    all_to_all x1, blocking collectives, local(): lax.all_to_all(gated, 'head', split_axis=0, concat_axis=1, tiled=True)  27.2 us
    unnamed x19, local copies, waits for them, and re-layouts  16.6 us
    ppermute x2, waiting for transfers between devices, with_halo(): lax.ppermute(lax.slice_in_dim(block, block.shape[dim] - width, None, axis...  13.2 us
    reshape x1, local copies, waits for them, and re-layouts, local(): widened = widened.reshape(2, 3 * cache_tiles, TILE, heads_here, HD)  10.8 us
    all_to_all x1, waiting for transfers between devices, local(): lax.all_to_all(jnp.stack(jnp.split(keys, lax.axis_size('head'), axis=1)),...  10.7 us
    reshape x4, local copies, waits for them, and re-layouts, group_blocks(): return window.reshape(2, 5, TILE, heads_here, HD)  9.41 us
  transfers between devices with their start and end apart: 7, of which 3 were waited for; matrix products, arithmetic and copies ran while one was open for 9% of the time, Pallas kernels for 0%

profile of v1, /device:TPU:256, one launch (start us, length us, event | category | flops | bytes accessed | tf_op | source)
XLA Modules:
  0.0 337.9 jit_solution(13195144934840607314)
XLA Ops:
  0.0 1.6 bitcast_dynamic-update-slice_fusion.9
  11.5 3.6 %all-to-all-start = ((bf16[8,32,768]{2,1,0:T(8,128)(2,1)}), bf16[8,32,768]{2,1,0:T(8,128)(2,1)S(1)}, u32[]{:S(2)}, u32[]{:S(2)}) async-start(bf16[8,32,768]{2,1,0:T(8,128)(2,1)} %bitcast_dynamic-update-slice_fusion.2), calls=%async_computation | async-start | bytes 786432 | tf_op jit(solution)/shard_map/all_to_all | solution.py:54
  15.1 1.8 copy.74
  16.9 10.7 %all-to-all-done = bf16[8,32,768]{2,1,0:T(8,128)(2,1)S(1)} async-done(((bf16[8,32,768]{2,1,0:T(8,128)(2,1)}), bf16[8,32,768]{2,1,0:T(8,128)(2,1)S(1)}, u32[]{:S(2)}, u32[]{:S(2)}) %all-to-all-start) | async-done | bytes 393248 | tf_op jit(solution)/shard_map/all_to_all | solution.py:54
  27.5 3.5 %all-to-all-start.1 = ((bf16[32,8,768]{2,0,1:T(8,128)(2,1)}), bf16[32,8,768]{2,0,1:T(8,128)(2,1)S(1)}, u32[]{:S(2)}, u32[]{:S(2)}) async-start(bf16[32,8,768]{2,0,1:T(8,128)(2,1)} %bitcast.80), calls=%async_computation.1 | async-start | bytes 786432 | tf_op jit(solution)/shard_map/all_to_all | solution.py:57
  32.3 3.5 %collective-permute-start.2 = (bf16[2,512,768]{2,1,0:T(8,128)(2,1)}, bf16[2,512,768]{2,1,0:T(8,128)(2,1)}, u32[]{:S(2)}, u32[]{:S(2)}) collective-permute-start(bf16[2,512,768]{2,1,0:T(8,128)(2,1)} %pad_maximum_fusion.3), channel_id=1, source_target_pairs={{0,8},{8,16},{16,24},{24,32},{32,40},{40,48},{48,56},{56,64},{64,7... | collective-permute-start | bytes 4718600 | tf_op jit(solution)/shard_map/ppermute | solution.py:17
  35.8 10.5 %collective-permute-start.3 = (bf16[2,512,768]{2,1,0:T(8,128)(2,1)}, bf16[2,512,768]{2,1,0:T(8,128)(2,1)}, u32[]{:S(2)}, u32[]{:S(2)}) collective-permute-start(bf16[2,512,768]{2,1,0:T(8,128)(2,1)} %pad_maximum_fusion.3), channel_id=1, source_target_pairs={{8,0},{16,8},{24,16},{32,24},{40,32},{48,40},{56,48},{64,56},{72,6... | collective-permute-start | bytes 4718600 | tf_op jit(solution)/shard_map/ppermute | solution.py:20
  47.1 5.0 %all-to-all-start.2 = ((bf16[32,8,768]{2,0,1:T(8,128)(2,1)}), bf16[32,8,768]{2,0,1:T(8,128)(2,1)S(1)}, u32[]{:S(2)}, u32[]{:S(2)}) async-start(bf16[32,8,768]{2,0,1:T(8,128)(2,1)} %bitcast.79), calls=%async_computation.2 | async-start | bytes 786432 | tf_op jit(solution)/shard_map/all_to_all | solution.py:52
  54.1 1.9 collective-permute-start
  56.0 37.1 %collective-permute-start.1 = (bf16[2,256,768]{2,1,0:T(8,128)(2,1)}, bf16[2,256,768]{2,1,0:T(8,128)(2,1)}, u32[]{:S(2)}, u32[]{:S(2)}) collective-permute-start(bf16[2,256,768]{2,1,0:T(8,128)(2,1)} %pad_maximum_fusion.4), channel_id=1, source_target_pairs={{8,0},{16,8},{24,16},{32,24},{40,32},{48,40},{56,48},{64,56},{72,6... | collective-permute-start | bytes 2359304 | tf_op jit(solution)/shard_map/ppermute | solution.py:20
  93.2 128.9 %collective-permute-done.3 = bf16[2,512,768]{2,1,0:T(8,128)(2,1)} collective-permute-done((bf16[2,512,768]{2,1,0:T(8,128)(2,1)}, bf16[2,512,768]{2,1,0:T(8,128)(2,1)}, u32[]{:S(2)}, u32[]{:S(2)}) %collective-permute-start.3) | collective-permute-done | bytes 1572896 | tf_op jit(solution)/shard_map/ppermute | solution.py:20
  222.2 4.9 %pad_maximum_fusion.1 = bf16[2,1536,768]{2,1,0:T(8,128)(2,1)} fusion(bf16[2,512,768]{2,1,0:T(8,128)(2,1)} %collective-permute-done.3, bf16[1,512,768]{2,1,0:T(8,128)(2,1)S(1)} %bitcast.122, bf16[1,512,768]{2,1,0:T(8,128)(2,1)S(1)} %bitcast.124, bf16[2,512,768]{2,1,0:T(8,128)(2,1)} %collective-permute-done.2), kind=kLoop, calls=%fused_computation.38 | loop fusion | flops 18874368 | bytes 9437184 | tf_op jit(solution)/shard_map/concatenate | solution.py:21
  227.1 10.8 %reshape.78 = bf16[2,12,128,6,128]{4,3,2,1,0:T(8,128)(2,1)} reshape(bf16[2,1536,768]{2,1,0:T(8,128)(2,1)} %pad_maximum_fusion.1) | data formatting | bytes 9437184 | tf_op jit(solution)/shard_map/reshape | solution.py:87
  237.8 6.4 %copy.55 = bf16[2,12,128,6,128]{4,2,3,1,0:T(8,128)(2,1)} copy(bf16[2,12,128,6,128]{4,3,2,1,0:T(8,128)(2,1)} %reshape.78) | data formatting | bytes 9437184
  244.3 13.2 %collective-permute-done = bf16[2,256,768]{2,1,0:T(8,128)(2,1)} collective-permute-done((bf16[2,256,768]{2,1,0:T(8,128)(2,1)}, bf16[2,256,768]{2,1,0:T(8,128)(2,1)}, u32[]{:S(2)}, u32[]{:S(2)}) %collective-permute-start) | collective-permute-done | bytes 786464 | tf_op jit(solution)/shard_map/ppermute | solution.py:17
  257.5 3.0 pad_maximum_fusion.2
  260.5 47.6 %while.17 = (s32[]{:T(128)}, f32[2,128,6,128]{1,3,2,0:T(8,128)}, f32[2,6,128]{2,1,0:T(8,128)S(1)}, f32[2,6,128]{2,1,0:T(8,128)S(1)}, s32[2]{0:T(128)S(1)}, /*ind...) while((s32[]{:T(128)}, f32[2,128,6,128]{1,3,2,0:T(8,128)}, ...), condition=%wide.region_3.4_spmd.clone, body=%wide.region_0.3_spmd.clone.sunk | while | flops 465272384 | bytes 78874744 | solution.py:96
  263.2 3.2 gather_fusion
  268.5 2.9 constant_dynamic-slice_fusion.6
  271.4 4.2 %reshape.101 = bf16[2,5,128,6,128]{4,3,2,1,0:T(8,128)(2,1)S(1)} reshape(bf16[2,640,768]{2,1,0:T(8,128)(2,1)} %constant_dynamic-slice_fusion.6) | data formatting | bytes 3932160 | tf_op jit(solution)/shard_map/while/body/eval_jaxpr/reshape | solution.py:84
  287.0 3.2 gather_fusion
  292.3 2.9 constant_dynamic-slice_fusion.6
  295.2 4.2 %reshape.101 = bf16[2,5,128,6,128]{4,3,2,1,0:T(8,128)(2,1)S(1)} reshape(bf16[2,640,768]{2,1,0:T(8,128)(2,1)} %constant_dynamic-slice_fusion.6) | data formatting | bytes 3932160 | tf_op jit(solution)/shard_map/while/body/eval_jaxpr/reshape | solution.py:84
  310.0 27.2 %all_to_all.56 = bf16[8,32,768]{2,1,0:T(8,128)(2,1)S(1)} all-to-all(bf16[8,32,768]{2,1,0:T(8,128)(2,1)S(1)} %multiply_convert_fusion), channel_id=1, replica_groups=mesh['ctx'=64,'head'=8] {'head'}, dimensions={0} | all-to-all | bytes 786432 | tf_op jit(solution)/shard_map/all_to_all | solution.py:99
  (101 shorter events, 37.9 us)
Async XLA Ops:
  0.0 52.1 %copy-start = (s32[128,4]{0,1:T(4,128)S(1)}, s32[128,4]{0,1:T(4,128)}, u32[]{:S(2)}) copy-start(s32[128,4]{0,1:T(4,128)} %param.15) | copy-start | bytes 6148
  0.0 31.0 %copy-start.6 = (bf16[512,768]{1,0:T(8,128)(2,1)S(1)}, bf16[512,768]{1,0:T(8,128)(2,1)}, u32[]{:S(2)}) copy-start(bf16[512,768]{1,0:T(8,128)(2,1)} %param.13) | copy-start | bytes 2359300
  0.0 31.0 %copy-start.5 = (bf16[512,768]{1,0:T(8,128)(2,1)S(1)}, bf16[512,768]{1,0:T(8,128)(2,1)}, u32[]{:S(2)}) copy-start(bf16[512,768]{1,0:T(8,128)(2,1)} %param.14) | copy-start | bytes 2359300
  0.0 46.3 %copy-start.9 = (bf16[32,6144]{1,0:T(8,128)(2,1)S(1)}, bf16[32,6144]{1,0:T(8,128)(2,1)}, u32[]{:S(2)}) copy-start(bf16[32,6144]{1,0:T(8,128)(2,1)} %param.10) | copy-start | bytes 1179652
  11.5 40.8 %copy-start.10 = (s32[128]{0:T(128)S(1)}, s32[128]{0:T(128)}, u32[]{:S(2)}) copy-start(s32[128]{0:T(128)} %param.16) | copy-start | bytes 1540
  11.5 16.0 %all-to-all-start = ((bf16[8,32,768]{2,1,0:T(8,128)(2,1)}), bf16[8,32,768]{2,1,0:T(8,128)(2,1)S(1)}, u32[]{:S(2)}, u32[]{:S(2)}) async-start(bf16[8,32,768]{2,1,0:T(8,128)(2,1)} %bitcast_dynamic-update-slice_fusion.2), calls=%async_computation | async-start | bytes 786432 | tf_op jit(solution)/shard_map/all_to_all | solution.py:54
  27.5 19.5 %all-to-all-start.1 = ((bf16[32,8,768]{2,0,1:T(8,128)(2,1)}), bf16[32,8,768]{2,0,1:T(8,128)(2,1)S(1)}, u32[]{:S(2)}, u32[]{:S(2)}) async-start(bf16[32,8,768]{2,0,1:T(8,128)(2,1)} %bitcast.80), calls=%async_computation.1 | async-start | bytes 786432 | tf_op jit(solution)/shard_map/all_to_all | solution.py:57
  32.3 60.9 %collective-permute-start.2 = (bf16[2,512,768]{2,1,0:T(8,128)(2,1)}, bf16[2,512,768]{2,1,0:T(8,128)(2,1)}, u32[]{:S(2)}, u32[]{:S(2)}) collective-permute-start(bf16[2,512,768]{2,1,0:T(8,128)(2,1)} %pad_maximum_fusion.3), channel_id=1, source_target_pairs={{0,8},{8,16},{16,24},{24,32},{32,40},{40,48},{48,56},{56,64},{64,7... | collective-permute-start | bytes 4718600 | tf_op jit(solution)/shard_map/ppermute | solution.py:17
  35.8 186.4 %collective-permute-start.3 = (bf16[2,512,768]{2,1,0:T(8,128)(2,1)}, bf16[2,512,768]{2,1,0:T(8,128)(2,1)}, u32[]{:S(2)}, u32[]{:S(2)}) collective-permute-start(bf16[2,512,768]{2,1,0:T(8,128)(2,1)} %pad_maximum_fusion.3), channel_id=1, source_target_pairs={{8,0},{16,8},{24,16},{32,24},{40,32},{48,40},{56,48},{64,56},{72,6... | collective-permute-start | bytes 4718600 | tf_op jit(solution)/shard_map/ppermute | solution.py:20
  47.1 213.4 %all-to-all-start.2 = ((bf16[32,8,768]{2,0,1:T(8,128)(2,1)}), bf16[32,8,768]{2,0,1:T(8,128)(2,1)S(1)}, u32[]{:S(2)}, u32[]{:S(2)}) async-start(bf16[32,8,768]{2,0,1:T(8,128)(2,1)} %bitcast.79), calls=%async_computation.2 | async-start | bytes 786432 | tf_op jit(solution)/shard_map/all_to_all | solution.py:52
  54.1 203.4 %collective-permute-start = (bf16[2,256,768]{2,1,0:T(8,128)(2,1)}, bf16[2,256,768]{2,1,0:T(8,128)(2,1)}, u32[]{:S(2)}, u32[]{:S(2)}) collective-permute-start(bf16[2,256,768]{2,1,0:T(8,128)(2,1)} %pad_maximum_fusion.4), channel_id=1, source_target_pairs={{0,8},{8,16},{16,24},{24,32},{32,40},{40,48},{48,56},{56,64},{64,7... | collective-permute-start | bytes 2359304 | tf_op jit(solution)/shard_map/ppermute | solution.py:17
  56.0 201.5 %collective-permute-start.1 = (bf16[2,256,768]{2,1,0:T(8,128)(2,1)}, bf16[2,256,768]{2,1,0:T(8,128)(2,1)}, u32[]{:S(2)}, u32[]{:S(2)}) collective-permute-start(bf16[2,256,768]{2,1,0:T(8,128)(2,1)} %pad_maximum_fusion.4), channel_id=1, source_target_pairs={{8,0},{16,8},{24,16},{32,24},{40,32},{48,40},{56,48},{64,56},{72,6... | collective-permute-start | bytes 2359304 | tf_op jit(solution)/shard_map/ppermute | solution.py:20
  275.6 1.8 copy-start.3
  276.2 1.3 copy-start.1
  279.8 1.5 copy-start.2
  279.8 2.0 copy-start.4
  279.8 2.2 copy-start.7
  283.4 0.9 copy-start.8
  299.4 1.8 copy-start.3
  300.0 1.3 copy-start.1
  303.6 1.5 copy-start.2
  303.6 2.0 copy-start.4
  303.6 2.2 copy-start.7
  307.2 0.9 copy-start.8
